TPU v7x, 32 devices: a whole 2x2x4 slice. The times are simulated.
32 devices in a mesh: section: 2 (over core), dp: 4 (over y, x), tensor: 4 (over z).
Axes of the slice: x: 2, y: 2, z: 4, core: 2. Of those that a mesh axis runs over, the one named last changes fastest.
Arguments:
- hidden: bfloat16 [8, 128, 2, 4, 1024], P('dp', None, 'section', 'tensor'), may hold values from -6 to 6
- head_grad: bfloat16 [8, 128, 2, 4, 1024], P('dp', None, None, 'tensor'), may hold values from -6 to 6
- w_in: bfloat16 [2, 5120, 2, 4, 1024], P('section', None, None, 'tensor'), may hold values from -0.0625 to 0.0625
- w_out: bfloat16 [2, 4096, 2, 4, 1024], P('section', None, None, 'tensor'), may hold values from -0.09375 to 0.09375
- gain: float32 [2, 2, 4, 1024], P('section', None, 'tensor'), may hold values from 0.1 to 1.9
- dest_slot: int32 [8], replicated, may hold values from -1 to 7, as said below
- lengths: int32 [8], replicated, may hold values from 1 to 128, as said below
- advantage: int32 [8, 128], replicated, may hold values from -32 to 32
Outputs:
- grad_w_in: bfloat16 [2, 5120, 2, 4, 1024], P('section', 'dp', None, 'tensor')
- grad_w_out: bfloat16 [2, 4096, 2, 4, 1024], P('section', 'dp', None, 'tensor')
- grad_gain: float32 [2, 2, 4, 1024], P('section', None, 'tensor')
Inputs may be any that keep to these rules, and one draw needn't show every extreme that they name: `dest_slot`: each slot is named by at most one row, and the rows of one data group that are kept go to different data groups; a kept row keeps its place within its slot block, so row i goes to a slot j with j % 2 = i % 2. `lengths`: some row has all 128 tokens live.
All inputs are finite; a program needn't handle non-finite values.
Results may differ from a plain program's by a relative error of at most 0.039.
Values may be sent and summed in bfloat16 or wider, within the bound.
No kernel may reach another device: no remote copies, remote signals or barrier semaphores. Data moves between devices by JAX's collectives and lax.ppermute only.
A program may use at most 576 MiB of HBM per device.

v0:
```python
import jax
import jax.numpy as jnp
from jax import lax
from jax.sharding import PartitionSpec as P

HD = 128

eps = 1e-06
adv_step = 0.0625
masked_score = -1e30

f32 = jnp.float32
bf16 = jnp.bfloat16


def shifted(value, axis, steps):
    count = lax.axis_size(axis)
    return lax.ppermute(value, axis, [(i, (i + steps) % count) for i in range(count)])


def swap(value):
    return shifted(value, "section", 1)


def gathered_list(value, axis):
    return [value] + [shifted(value, axis, d) for d in range(1, lax.axis_size(axis))]


def scattered_list(chunk_of, axis):
    count = lax.axis_size(axis)
    me = lax.axis_index(axis)
    return [chunk_of(me)] + [
        shifted(chunk_of(lax.rem(me + d, count)), axis, d) for d in range(1, count)
    ]


def small_sum(value, axis):
    total = value
    for piece in gathered_list(value, axis)[1:]:
        total = total + piece
    return total


def contract_rows(first, second):
    return lax.dot_general(first, second, (((0,), (0,)), ((), ())), preferred_element_type=f32)


def contract_cols(first, second):
    return lax.dot_general(first, second, (((1,), (1,)), ((), ())), preferred_element_type=f32)


def settle(amount):
    return lax.optimization_barrier(amount.astype(bf16)).astype(f32)


def shards(hidden, head_grad, w_in, w_out, gain, dest_slot, lengths, advantage):
    sections = lax.axis_size("section")
    groups = lax.axis_size("dp")
    tensors = lax.axis_size("tensor")
    sec = lax.axis_index("section")
    grp = lax.axis_index("dp")
    ten = lax.axis_index("tensor")
    assert sections == 2
    rows, length, feat = hidden.shape[0], hidden.shape[1], hidden.shape[4]
    width = sections * tensors * feat
    qkv_width = w_in.shape[1]
    out_width = w_out.shape[1]
    total_heads = out_width // HD
    kv_total = (qkv_width - out_width) // (2 * HD)
    group_size = total_heads // kv_total
    heads = total_heads // tensors
    kv_local = max(1, heads // group_size)
    per_share = heads // kv_local
    sharers = tensors * kv_local // kv_total
    q_cols, kv_cols = heads * HD, kv_local * HD
    per = rows // sections
    own, both = per * length, rows * length
    in_rows, out_rows = qkv_width // groups, out_width // groups
    score_scale = HD ** (-0.5)

    order = jnp.concatenate(
        [sec * per + jnp.arange(per), (1 - sec) * per + jnp.arange(per)]
    ).astype(jnp.int32)
    slot_ids = grp * rows + order
    matches = dest_slot[None, :] == slot_ids[:, None]
    slot_live = jnp.any(matches, axis=1)
    slot_len = jnp.maximum(jnp.sum(jnp.where(matches, lengths[None, :], 0), axis=1), 1)
    slot_adv = jnp.sum(jnp.where(matches[:, :, None], advantage[None, :, :], 0), axis=1)
    positions = jnp.arange(length, dtype=jnp.int32)

    def own_first(value):
        return jnp.concatenate(
            [
                lax.dynamic_slice_in_dim(value, sec * per, per),
                lax.dynamic_slice_in_dim(value, (1 - sec) * per, per),
            ]
        )

    blocks = gathered_list(own_first(hidden.reshape(rows, length, feat)), "dp")
    routed = jnp.zeros((rows, length, feat), bf16)
    for d, block in enumerate(blocks):
        source = lax.rem(grp + groups - d, groups)
        hit = dest_slot[source * rows + order] == slot_ids
        routed = jnp.where(hit[:, None, None], block, routed)
    entry = routed.reshape(both, feat)

    def halves(weights):
        flat = weights.reshape(weights.shape[1], sections, feat)
        first, second = flat[:, 0], flat[:, 1]
        kept = jnp.where(sec == 0, first, second)
        sent = jnp.where(sec == 0, second, first)
        return kept, swap(sent)

    win_kept, win_got = halves(w_in)
    wout_kept, wout_got = halves(w_out)
    gain_kept, gain_got = (value.reshape(feat) for value in halves(gain[:, None]))

    def with_weights(layer, function, kept, got):
        return lax.cond(sec == layer, lambda: function(kept), lambda: function(got))

    def gain_of(layer):
        return jnp.where(sec == layer, gain_kept, gain_got)

    token_keep = (positions[None, :] < slot_len[:, None]) & slot_live[:, None]
    factor = jnp.where(token_keep, slot_adv.astype(f32) * adv_step, 0.0)
    grad_half = lax.dynamic_index_in_dim(
        head_grad.reshape(rows, length, sections, feat), sec, 2, keepdims=False
    )
    seed = (own_first(grad_half).astype(f32) * factor[:, :, None]).astype(bf16).reshape(both, feat)

    own_len = slot_len[:per]
    allowed = (positions[None, None, :] <= positions[None, :, None]) & (
        positions[None, None, :] < own_len[:, None, None]
    )
    mask = allowed[:, None, None, :, :]

    def kv_start(index):
        return index * heads // group_size

    def head_sums(partial, chunk_of):
        summed = (partial[:own].astype(f32) + swap(partial[own:]).astype(f32)).astype(bf16)
        pieces = scattered_list(lambda index: chunk_of(summed, index), "tensor")
        total = pieces[0].astype(f32)
        for piece in pieces[1:]:
            total = total + piece.astype(f32)
        return total

    def qkv_chunk(value, index):
        return jnp.concatenate(
            [
                lax.dynamic_slice_in_dim(value, index * q_cols, q_cols, 1),
                lax.dynamic_slice_in_dim(value, out_width + kv_start(index) * HD, kv_cols, 1),
                lax.dynamic_slice_in_dim(
                    value, out_width + (kv_total + kv_start(index)) * HD, kv_cols, 1
                ),
            ],
            axis=1,
        )

    def out_chunk(value, index):
        return lax.dynamic_slice_in_dim(value, index * q_cols, q_cols, 1)

    def in_order(pieces):
        stacked = jnp.stack(pieces)
        return jnp.take(stacked, (ten - jnp.arange(tensors)) % tensors, axis=0)

    def forward_attention(hidden_in, layer):
        states = hidden_in.astype(f32)
        normed = (states * gain_of(layer)).astype(bf16)
        square = jnp.sum(states * states, axis=1)
        square = small_sum(square[:own] + swap(square[own:]), "tensor")
        inv_rms = lax.rsqrt(square / width + eps)
        partial = with_weights(
            layer, lambda w: contract_cols(normed, w).astype(bf16), win_kept, win_got
        )
        linear = head_sums(partial, qkv_chunk)
        scaled = (inv_rms[:, None] * linear).astype(bf16)
        queries = scaled[:, :q_cols].reshape(per, length, kv_local, per_share, HD)
        keys = scaled[:, q_cols : q_cols + kv_cols].reshape(per, length, kv_local, HD)
        values = scaled[:, q_cols + kv_cols :].reshape(per, length, kv_local, HD)
        scores = jnp.einsum("bikgd,bjkd->bkgij", queries, keys, preferred_element_type=f32)
        scores = jnp.where(mask, scores * score_scale, masked_score)
        terms = jnp.where(mask, jnp.exp(scores - jnp.max(scores, axis=-1, keepdims=True)), 0.0)
        attention = terms / jnp.sum(terms, axis=-1, keepdims=True)
        attended = jnp.einsum(
            "bkgij,bjkd->bikgd", attention.astype(bf16), values, preferred_element_type=f32
        )
        attended = attended.astype(bf16).reshape(own, q_cols)
        ordered = in_order(gathered_list(attended, "tensor"))
        gathered = ordered.transpose(1, 0, 2).reshape(own, out_width)
        return normed, inv_rms, linear, queries, keys, values, attention, gathered

    def head_grads(grad, layer):
        partial = with_weights(
            layer, lambda w: contract_cols(grad, w).astype(bf16), wout_kept, wout_got
        )
        return head_sums(partial, out_chunk).astype(bf16)

    def backward_attention(own_grad, saved):
        normed, inv_rms, linear, queries, keys, values, attention, gathered = saved
        grads = own_grad.reshape(per, length, kv_local, per_share, HD)
        d_prob = jnp.einsum("bikgd,bjkd->bkgij", grads, values, preferred_element_type=f32)
        d_score = (
            attention * (d_prob - jnp.sum(attention * d_prob, axis=-1, keepdims=True)) * score_scale
        ).astype(bf16)
        d_query = jnp.einsum("bkgij,bjkd->bikgd", d_score, keys, preferred_element_type=f32)
        d_query = d_query.astype(bf16).reshape(own, q_cols).astype(f32)
        d_key = jnp.einsum("bkgij,bikgd->bjkgd", d_score, queries, preferred_element_type=f32)
        d_value = jnp.einsum(
            "bkgij,bikgd->bjkgd", attention.astype(bf16), grads, preferred_element_type=f32
        )
        d_key = jnp.sum(settle(d_key), axis=3).reshape(own, kv_cols)
        d_value = jnp.sum(settle(d_value), axis=3).reshape(own, kv_cols)
        d_linear = jnp.concatenate([d_query, d_key, d_value], axis=1)
        d_scale = small_sum(jnp.sum(d_linear * linear, axis=1), "tensor")
        coefficient = d_scale * inv_rms**3 * (-1.0 / width)
        coefficient = jnp.concatenate([coefficient, swap(coefficient)])
        low = (inv_rms[:, None] * d_linear).astype(bf16)
        ordered = in_order(gathered_list(low, "tensor"))

        def kv_part(start):
            part = ordered[:, :, start : start + kv_cols]
            if sharers > 1:
                part = part.reshape(kv_total, sharers, own, HD)
                part = jnp.sum(part.astype(f32), axis=1).astype(bf16)
            return part.transpose(1, 0, 2).reshape(own, kv_total * HD)

        grad_low = jnp.concatenate(
            [
                ordered[:, :, :q_cols].transpose(1, 0, 2).reshape(own, out_width),
                kv_part(q_cols),
                kv_part(q_cols + kv_cols),
            ],
            axis=1,
        )
        return grad_low, coefficient

    def pair(value):
        return jnp.concatenate([value, swap(value)])

    def by_tokens(pieces):
        return jnp.concatenate([piece[:own] for piece in pieces] + [piece[own:] for piece in pieces])

    def weight_grad(left, right_pieces, block):
        pieces = scattered_list(
            lambda index: lax.dynamic_slice_in_dim(left, index * block, block, 1), "dp"
        )
        return contract_rows(pair(jnp.concatenate(pieces)), by_tokens(right_pieces)).astype(bf16)

    saved_0 = forward_attention(entry, 0)
    out_all = pair(saved_0[-1])
    update = with_weights(
        0, lambda w: jnp.dot(out_all, w, preferred_element_type=f32), wout_kept, wout_got
    )
    hidden_1 = (entry.astype(f32) + update).astype(bf16)
    saved_1 = forward_attention(hidden_1, 1)

    def backward_layer(grad, hidden_in, saved, layer):
        own_grad = head_grads(grad, layer)
        grad_low, coefficient = backward_attention(own_grad, saved)
        grad_all = pair(grad_low)
        grad_normed = with_weights(
            layer, lambda w: jnp.dot(grad_all, w, preferred_element_type=f32), win_kept, win_got
        )
        states = hidden_in.astype(f32)
        grad_prev = (
            grad.astype(f32) + grad_normed * gain_of(layer) + coefficient[:, None] * states
        ).astype(bf16)
        gain_term = small_sum(jnp.sum(grad_normed * states, axis=0), "dp")
        in_grad = weight_grad(grad_low, gathered_list(saved[0], "dp"), in_rows)
        out_grad = weight_grad(saved[-1], gathered_list(grad, "dp"), out_rows)
        return grad_prev, in_grad, out_grad, gain_term

    grad_1, in_1, out_1, gain_1 = backward_layer(seed, hidden_1, saved_1, 1)
    _, in_0, out_0, gain_0 = backward_layer(grad_1, entry, saved_0, 0)

    def placed(layer_0, layer_1):
        to_second = lax.ppermute(layer_1, "section", [(0, 1)])
        to_first = lax.ppermute(layer_0, "section", [(1, 0)])
        first = jnp.where(sec == 0, layer_0, to_second)
        second = jnp.where(sec == 0, to_first, layer_1)
        return first, second

    def shaped(layer_0, layer_1, count):
        return jnp.stack(placed(layer_0, layer_1), axis=1).reshape(1, count, sections, 1, feat)

    grad_gain = jnp.stack(placed(gain_0, gain_1)).reshape(1, sections, 1, feat)
    return (shaped(in_0, in_1, in_rows), shaped(out_0, out_1, out_rows), grad_gain)


def solution(mesh):
    placed = (
        P("dp", None, "section", "tensor", None),
        P("dp", None, None, "tensor", None),
        P("section", None, None, "tensor", None),
        P("section", None, None, "tensor", None),
        P("section", None, "tensor", None),
        P(),
        P(),
        P(),
    )
    return jax.shard_map(
        shards,
        mesh=mesh,
        in_specs=placed,
        out_specs=(
            P("section", "dp", None, "tensor", None),
            P("section", "dp", None, "tensor", None),
            P("section", None, "tensor", None),
        ),
        check_vma=False,
    )
```

profile of v0, /device:TPU:11, one launch (start us, length us, event | category | flops | bytes accessed | tf_op | source)
XLA Modules:
  0.0 649.6 jit_solution(8298343150105153045)
XLA Ops:
  0.6 20.4 %copy.232 = bf16[1,5120,2,1,1024]{4,1,2,3,0:T(8,128)(2,1)} copy(bf16[1,5120,2,1,1024]{4,2,3,1,0:T(2,128)(2,1)} %param.28) | data formatting | bytes 41943040 | tf_op args[2]
  21.0 15.7 %select_bitcast_fusion = (bf16[5120,1024]{1,0:T(8,128)(2,1)}, bf16[5120,1024]{1,0:T(8,128)(2,1)}) fusion(pred[]{:T(512)S(6)} %eq.76, bf16[5120,2,1024]{2,0,1:T(8,128)(2,1)} %bitcast.308), kind=kLoop, calls=%fused_computation.10 | loop fusion | flops 10485760 | bytes 41943040 | tf_op jit(solution)/shard_map/jit(_where)/select_n | solution.py:110
  39.8 11.1 %copy.233 = bf16[1,4096,2,1,1024]{4,1,2,3,0:T(8,128)(2,1)S(1)} copy(bf16[1,4096,2,1,1024]{4,2,3,1,0:T(2,128)(2,1)} %param.29) | data formatting | bytes 33554432 | tf_op args[3]
  68.9 9.2 %collective-permute-done.2 = bf16[2,128,1024]{2,1,0:T(8,128)(2,1)S(1)} collective-permute-done((bf16[2,128,1024]{2,1,0:T(8,128)(2,1)S(1)}, bf16[2,128,1024]{2,1,0:T(8,128)(2,1)S(1)}, u32[]{:S(2)}, u32[]{:S(2)}) %collective-permute-start.2) | collective-permute-done | bytes 524320 | tf_op jit(solution)/shard_map/ppermute | solution.py:18
  104.1 12.4 %conditional.11 = (bf16[256,5120]{1,0:T(8,128)(2,1)}) conditional(s32[]{:T(128)} %convert_element_type.344, (bf16[256,1024]{1,0:T(8,128)(2,1)S(1)}, bf16[5120,1024]{1,0:T(8,128)(2,1)}) %tuple.64, (bf16[256,1024]{1,0:T(8,128)(2,1)S(1)}, bf16[5120,1024]{1,0:T(8,128)(2,1)}) %tuple.65), branch_computations={%region_1.2_spmd, %region_2.3_spmd} | conditional | flops 2684354560 | bytes 13631496
  104.1 12.2 %fusion.71 = bf16[256,5120]{1,0:T(8,128)(2,1)} fusion(bf16[256,1024]{1,0:T(8,128)(2,1)S(1)} %get-tuple-element.84, bf16[5120,1024]{1,0:T(8,128)(2,1)} %get-tuple-element.88), kind=kOutput, calls=%fused_computation.316 | convolution fusion | flops 2684354560 | bytes 13631488 | tf_op jit(solution)/shard_map/cond/branch_0_fun/dot_general | solution.py:49
  129.7 16.0 %collective-permute-done.50 = bf16[256,1024]{1,0:T(8,128)(2,1)S(1)} collective-permute-done((bf16[256,1024]{1,0:T(8,128)(2,1)S(1)}, bf16[256,1024]{1,0:T(8,128)(2,1)S(1)}, u32[]{:S(2)}, u32[]{:S(2)}) %collective-permute-start.50) | collective-permute-done | bytes 524320 | tf_op jit(solution)/shard_map/ppermute | solution.py:18
  155.3 7.3 %conditional.26 = (bf16[256,4096]{1,0:T(8,128)(2,1)}) conditional(s32[]{:T(128)} %convert_element_type.362, (bf16[256,1024]{1,0:T(8,128)(2,1)}, bf16[4096,1024]{1,0:T(8,128)(2,1)}) %tuple.70, (bf16[256,1024]{1,0:T(8,128)(2,1)}, bf16[4096,1024]{1,0:T(8,128)(2,1)}) %tuple.71), branch_computations={%region_15.17_spmd, %region_16.18_spmd} | conditional | flops 2147483648 | bytes 11010056
  155.3 7.3 %fusion.78 = bf16[256,4096]{1,0:T(8,128)(2,1)} fusion(bf16[256,1024]{1,0:T(8,128)(2,1)} %get-tuple-element.101, bf16[4096,1024]{1,0:T(8,128)(2,1)} %get-tuple-element.102), kind=kOutput, calls=%fused_computation.323 | convolution fusion | flops 2147483648 | bytes 11010048 | tf_op jit(solution)/shard_map/cond/branch_1_fun/dot_general | solution.py:49
  166.2 9.9 %collective-permute-done.11 = bf16[128,1280]{1,0:T(8,128)(2,1)} collective-permute-done((bf16[128,1280]{1,0:T(8,128)(2,1)S(1)}, bf16[128,1280]{1,0:T(8,128)(2,1)}, u32[]{:S(2)}, u32[]{:S(2)}) %collective-permute-start.11) | collective-permute-done | bytes 327712 | tf_op jit(solution)/shard_map/ppermute | solution.py:18
  192.4 13.5 %collective-permute-done.14 = bf16[128,1024]{0,1:T(8,128)(2,1)S(1)} collective-permute-done((bf16[128,1024]{0,1:T(8,128)(2,1)S(1)}, bf16[128,1024]{0,1:T(8,128)(2,1)S(1)}, u32[]{:S(2)}, u32[]{:S(2)}) %collective-permute-start.14) | collective-permute-done | bytes 262176 | tf_op jit(solution)/shard_map/ppermute | solution.py:18
  205.9 13.0 %collective-permute-done.15 = bf16[128,1024]{0,1:T(8,128)(2,1)S(1)} collective-permute-done((bf16[128,1024]{0,1:T(8,128)(2,1)S(1)}, bf16[128,1024]{0,1:T(8,128)(2,1)S(1)}, u32[]{:S(2)}, u32[]{:S(2)}) %collective-permute-start.15) | collective-permute-done | bytes 262176 | tf_op jit(solution)/shard_map/ppermute | solution.py:18
  257.2 12.2 %conditional.25 = (bf16[256,5120]{1,0:T(8,128)(2,1)}) conditional(s32[]{:T(128)} %convert_element_type.362, (bf16[256,1024]{1,0:T(8,128)(2,1)S(1)}, bf16[5120,1024]{1,0:T(8,128)(2,1)}) %tuple.68, (bf16[256,1024]{1,0:T(8,128)(2,1)S(1)}, bf16[5120,1024]{1,0:T(8,128)(2,1)}) %tuple.69), branch_computations={%region_11.13_spmd, %region_12.14_spmd} | conditional | flops 2684354560 | bytes 13631496
  257.2 12.2 %fusion.76 = bf16[256,5120]{1,0:T(8,128)(2,1)} fusion(bf16[256,1024]{1,0:T(8,128)(2,1)S(1)} %get-tuple-element.97, bf16[5120,1024]{1,0:T(8,128)(2,1)} %get-tuple-element.98), kind=kOutput, calls=%fused_computation.321 | convolution fusion | flops 2684354560 | bytes 13631488 | tf_op jit(solution)/shard_map/cond/branch_1_fun/dot_general | solution.py:49
  278.0 16.3 %collective-permute-done.57 = bf16[256,1024]{1,0:T(8,128)(2,1)S(1)} collective-permute-done((bf16[256,1024]{1,0:T(8,128)(2,1)S(1)}, bf16[256,1024]{1,0:T(8,128)(2,1)S(1)}, u32[]{:S(2)}, u32[]{:S(2)}) %collective-permute-start.57) | collective-permute-done | bytes 524320 | tf_op jit(solution)/shard_map/ppermute | solution.py:18
  304.1 18.4 %collective-permute-done.24 = bf16[128,1280]{1,0:T(8,128)(2,1)S(1)} collective-permute-done((bf16[128,1280]{1,0:T(8,128)(2,1)S(1)}, bf16[128,1280]{1,0:T(8,128)(2,1)S(1)}, u32[]{:S(2)}, u32[]{:S(2)}) %collective-permute-start.24) | collective-permute-done | bytes 327712 | tf_op jit(solution)/shard_map/ppermute | solution.py:18
  359.8 8.7 %collective-permute-done.69 = bf16[128,1024]{0,1:T(8,128)(2,1)} collective-permute-done((bf16[128,1024]{0,1:T(8,128)(2,1)}, bf16[128,1024]{0,1:T(8,128)(2,1)}, u32[]{:S(2)}, u32[]{:S(2)}) %collective-permute-start.69) | collective-permute-done | bytes 262176 | tf_op jit(solution)/shard_map/ppermute | solution.py:18
  368.6 18.5 %collective-permute-done.70 = bf16[128,1024]{0,1:T(8,128)(2,1)S(1)} collective-permute-done((bf16[128,1024]{0,1:T(8,128)(2,1)}, bf16[128,1024]{0,1:T(8,128)(2,1)S(1)}, u32[]{:S(2)}, u32[]{:S(2)}) %collective-permute-start.70) | collective-permute-done | bytes 262176 | tf_op jit(solution)/shard_map/ppermute | solution.py:18
  426.5 7.6 %collective-permute-done.54 = bf16[128,1280]{0,1:T(8,128)(2,1)S(1)} collective-permute-done((bf16[128,1280]{0,1:T(8,128)(2,1)S(1)}, bf16[128,1280]{0,1:T(8,128)(2,1)S(1)}, u32[]{:S(2)}, u32[]{:S(2)}) %collective-permute-start.54) | collective-permute-done | bytes 327712 | tf_op jit(solution)/shard_map/ppermute | solution.py:18
  497.1 8.0 %collective-permute-done.40 = bf16[128,1024]{1,0:T(8,128)(2,1)S(1)} collective-permute-done((bf16[128,1024]{1,0:T(8,128)(2,1)S(1)}, bf16[128,1024]{1,0:T(8,128)(2,1)S(1)}, u32[]{:S(2)}, u32[]{:S(2)}) %collective-permute-start.40) | collective-permute-done | bytes 262176 | tf_op jit(solution)/shard_map/ppermute | solution.py:18
  505.1 8.8 %collective-permute-done.41 = bf16[128,1024]{1,0:T(8,128)(2,1)S(1)} collective-permute-done((bf16[128,1024]{1,0:T(8,128)(2,1)S(1)}, bf16[128,1024]{1,0:T(8,128)(2,1)S(1)}, u32[]{:S(2)}, u32[]{:S(2)}) %collective-permute-start.41) | collective-permute-done | bytes 262176 | tf_op jit(solution)/shard_map/ppermute | solution.py:18
  524.5 19.2 %collective-permute-done.43 = bf16[128,1280]{1,0:T(8,128)(2,1)S(1)} collective-permute-done((bf16[128,1280]{1,0:T(8,128)(2,1)S(1)}, bf16[128,1280]{1,0:T(8,128)(2,1)S(1)}, u32[]{:S(2)}, u32[]{:S(2)}) %collective-permute-start.43) | collective-permute-done | bytes 327712 | tf_op jit(solution)/shard_map/ppermute | solution.py:18
  552.7 8.9 %collective-permute-start.45 = (bf16[128,1280]{0,1:T(8,128)(2,1)S(1)}, bf16[128,1280]{0,1:T(8,128)(2,1)S(1)}, u32[]{:S(2)}, u32[]{:S(2)}) collective-permute-start(bf16[128,1280]{0,1:T(8,128)(2,1)S(1)} %get-tuple-element.187), channel_id=1, source_target_pairs={{0,4},{4,8},{8,12},{12,0},{1,5},{5,9},{9,13},{13,1},{2,6},{6,10},{... | collective-permute-start | bytes 983048 | tf_op jit(solution)/shard_map/ppermute | solution.py:18
  630.7 18.5 %copy.175 = bf16[1,1280,2,1,1024]{4,2,3,1,0:T(2,128)(2,1)} copy(bf16[1,1280,2,1,1024]{4,1,2,3,0:T(8,128)(2,1)S(1)} %maximum_bitcast_fusion) | data formatting | bytes 10485760
  (523 shorter events, 396.0 us)
Async XLA Ops:
  36.8 67.3 %collective-permute-start.8 = (bf16[5120,1024]{1,0:T(8,128)(2,1)}, bf16[5120,1024]{1,0:T(8,128)(2,1)}, u32[]{:S(2)}, u32[]{:S(2)}) collective-permute-start(bf16[5120,1024]{1,0:T(8,128)(2,1)} %get-tuple-element.175), channel_id=1, source_target_pairs={{0,16},{16,0},{1,17},{17,1},{2,18},{18,2},{3,19},{19,3},{4,20},{20... | collective-permute-start | bytes 31457288 | tf_op jit(solution)/shard_map/ppermute | solution.py:18
  37.5 30.8 %collective-permute-start = (bf16[2,128,1024]{2,1,0:T(8,128)(2,1)S(1)}, bf16[2,128,1024]{2,1,0:T(8,128)(2,1)}, u32[]{:S(2)}, u32[]{:S(2)}) collective-permute-start(bf16[2,128,1024]{2,1,0:T(8,128)(2,1)S(1)} %pad_maximum_fusion.14), channel_id=1, source_target_pairs={{0,12},{4,0},{8,4},{12,8},{1,13},{5,1},{9,5},{13,9},{2,14},{6,2},{... | collective-permute-start | bytes 1572872 | tf_op jit(solution)/shard_map/ppermute | solution.py:18
  37.9 30.5 %collective-permute-start.1 = (bf16[2,128,1024]{2,1,0:T(8,128)(2,1)S(1)}, bf16[2,128,1024]{2,1,0:T(8,128)(2,1)}, u32[]{:S(2)}, u32[]{:S(2)}) collective-permute-start(bf16[2,128,1024]{2,1,0:T(8,128)(2,1)S(1)} %pad_maximum_fusion.14), channel_id=1, source_target_pairs={{0,8},{4,12},{8,0},{12,4},{1,9},{5,13},{9,1},{13,5},{2,10},{6,14},... | collective-permute-start | bytes 1572872 | tf_op jit(solution)/shard_map/ppermute | solution.py:18
  57.2 98.1 %collective-permute-start.17 = (bf16[4096,1024]{1,0:T(8,128)(2,1)}, bf16[4096,1024]{1,0:T(8,128)(2,1)}, u32[]{:S(2)}, u32[]{:S(2)}) collective-permute-start(bf16[4096,1024]{1,0:T(8,128)(2,1)} %get-tuple-element.177), channel_id=1, source_target_pairs={{0,16},{16,0},{1,17},{17,1},{2,18},{18,2},{3,19},{19,3},{4,20},{20... | collective-permute-start | bytes 25165832 | tf_op jit(solution)/shard_map/ppermute | solution.py:18
  89.4 38.6 %collective-permute-start.49 = (bf16[256,1024]{1,0:T(8,128)(2,1)S(1)}, bf16[256,1024]{1,0:T(8,128)(2,1)}, u32[]{:S(2)}, u32[]{:S(2)}) collective-permute-start(bf16[256,1024]{1,0:T(8,128)(2,1)S(1)} %fusion.19), channel_id=1, source_target_pairs={{0,4},{4,8},{8,12},{12,0},{1,5},{5,9},{9,13},{13,1},{2,6},{6,10},{... | collective-permute-start | bytes 1572872 | tf_op jit(solution)/shard_map/ppermute | solution.py:18
  118.0 29.2 %collective-permute-start.9 = (bf16[128,5120]{1,0:T(8,128)(2,1)S(1)}, bf16[128,5120]{1,0:T(8,128)(2,1)S(1)}, u32[]{:S(2)}, u32[]{:S(2)}) collective-permute-start(bf16[128,5120]{1,0:T(8,128)(2,1)S(1)} %slice.289), channel_id=1, source_target_pairs={{0,16},{16,0},{1,17},{17,1},{2,18},{18,2},{3,19},{19,3},{4,20},{20... | collective-permute-start | bytes 3932168 | tf_op jit(solution)/shard_map/ppermute | solution.py:18
  148.9 27.3 %collective-permute-start.11 = (bf16[128,1280]{1,0:T(8,128)(2,1)S(1)}, bf16[128,1280]{1,0:T(8,128)(2,1)}, u32[]{:S(2)}, u32[]{:S(2)}) collective-permute-start(bf16[128,1280]{1,0:T(8,128)(2,1)S(1)} %pad_maximum_fusion.16), channel_id=1, source_target_pairs={{0,2},{1,3},{2,0},{3,1},{4,6},{5,7},{6,4},{7,5},{8,10},{9,11},{10,... | collective-permute-start | bytes 983048 | tf_op jit(solution)/shard_map/ppermute | solution.py:18
  184.6 34.3 %collective-permute-start.15 = (bf16[128,1024]{0,1:T(8,128)(2,1)S(1)}, bf16[128,1024]{0,1:T(8,128)(2,1)S(1)}, u32[]{:S(2)}, u32[]{:S(2)}) collective-permute-start(bf16[128,1024]{0,1:T(8,128)(2,1)S(1)} %bitcast.341), channel_id=1, source_target_pairs={{0,3},{1,0},{2,1},{3,2},{4,7},{5,4},{6,5},{7,6},{8,11},{9,8},{10,9... | collective-permute-start | bytes 786440 | tf_op jit(solution)/shard_map/ppermute | solution.py:18
  188.1 38.2 %collective-permute-start.27 = (bf16[128,1024]{1,0:T(8,128)(2,1)}, bf16[128,1024]{1,0:T(8,128)(2,1)}, u32[]{:S(2)}, u32[]{:S(2)}) collective-permute-start(bf16[128,1024]{1,0:T(8,128)(2,1)} %get-tuple-element.231), channel_id=1, source_target_pairs={{0,1},{1,2},{2,3},{3,0},{4,5},{5,6},{6,7},{7,4},{8,9},{9,10},{10,1... | collective-permute-start | bytes 786440 | tf_op jit(solution)/shard_map/ppermute | solution.py:18
  189.3 38.0 %collective-permute-start.28 = (bf16[128,1024]{1,0:T(8,128)(2,1)}, bf16[128,1024]{1,0:T(8,128)(2,1)}, u32[]{:S(2)}, u32[]{:S(2)}) collective-permute-start(bf16[128,1024]{1,0:T(8,128)(2,1)} %get-tuple-element.233), channel_id=1, source_target_pairs={{0,2},{1,3},{2,0},{3,1},{4,6},{5,7},{6,4},{7,5},{8,10},{9,11},{10,... | collective-permute-start | bytes 786440 | tf_op jit(solution)/shard_map/ppermute | solution.py:18
  241.5 33.1 %collective-permute-start.64 = (bf16[512,1024]{1,0:T(8,128)(2,1)}, bf16[512,1024]{1,0:T(8,128)(2,1)}, u32[]{:S(2)}, u32[]{:S(2)}) collective-permute-start(bf16[512,1024]{1,0:T(8,128)(2,1)} %pad_maximum_fusion.10), channel_id=1, source_target_pairs={{0,16},{16,0},{1,17},{17,1},{2,18},{18,2},{3,19},{19,3},{4,20},{20... | collective-permute-start | bytes 3145736 | tf_op jit(solution)/shard_map/ppermute | solution.py:18
  300.5 27.5 %collective-permute-start.25 = (bf16[128,1280]{1,0:T(8,128)(2,1)S(1)}, bf16[128,1280]{1,0:T(8,128)(2,1)S(1)}, u32[]{:S(2)}, u32[]{:S(2)}) collective-permute-start(bf16[128,1280]{1,0:T(8,128)(2,1)S(1)} %pad_maximum_fusion.20), channel_id=1, source_target_pairs={{0,3},{1,0},{2,1},{3,2},{4,7},{5,4},{6,5},{7,6},{8,11},{9,8},{10,9... | collective-permute-start | bytes 983048 | tf_op jit(solution)/shard_map/ppermute | solution.py:18
  351.0 36.0 %collective-permute-start.70 = (bf16[128,1024]{0,1:T(8,128)(2,1)}, bf16[128,1024]{0,1:T(8,128)(2,1)S(1)}, u32[]{:S(2)}, u32[]{:S(2)}) collective-permute-start(bf16[128,1024]{0,1:T(8,128)(2,1)} %bitcast.112), channel_id=1, source_target_pairs={{0,3},{1,0},{2,1},{3,2},{4,7},{5,4},{6,5},{7,6},{8,11},{9,8},{10,9... | collective-permute-start | bytes 786440 | tf_op jit(solution)/shard_map/ppermute | solution.py:18
  351.1 42.5 %collective-permute-start.30 = (bf16[128,1280]{1,0:T(8,128)(2,1)}, bf16[128,1280]{1,0:T(8,128)(2,1)}, u32[]{:S(2)}, u32[]{:S(2)}) collective-permute-start(bf16[128,1280]{1,0:T(8,128)(2,1)} %get-tuple-element.237), channel_id=1, source_target_pairs={{0,1},{1,2},{2,3},{3,0},{4,5},{5,6},{6,7},{7,4},{8,9},{9,10},{10,1... | collective-permute-start | bytes 983048 | tf_op jit(solution)/shard_map/ppermute | solution.py:18
  357.7 39.1 %collective-permute-start.31 = (bf16[128,1280]{1,0:T(8,128)(2,1)}, bf16[128,1280]{1,0:T(8,128)(2,1)}, u32[]{:S(2)}, u32[]{:S(2)}) collective-permute-start(bf16[128,1280]{1,0:T(8,128)(2,1)} %get-tuple-element.237), channel_id=1, source_target_pairs={{0,2},{1,3},{2,0},{3,1},{4,6},{5,7},{6,4},{7,5},{8,10},{9,11},{10,... | collective-permute-start | bytes 983048 | tf_op jit(solution)/shard_map/ppermute | solution.py:18
  359.8 41.4 %collective-permute-start.32 = (bf16[128,1280]{1,0:T(8,128)(2,1)}, bf16[128,1280]{1,0:T(8,128)(2,1)}, u32[]{:S(2)}, u32[]{:S(2)}) collective-permute-start(bf16[128,1280]{1,0:T(8,128)(2,1)} %get-tuple-element.237), channel_id=1, source_target_pairs={{0,3},{1,0},{2,1},{3,2},{4,7},{5,4},{6,5},{7,6},{8,11},{9,8},{10,9... | collective-permute-start | bytes 983048 | tf_op jit(solution)/shard_map/ppermute | solution.py:18
  415.4 27.7 %collective-permute-start.33 = (bf16[128,5120]{0,1:T(8,128)(2,1)S(1)}, bf16[128,5120]{0,1:T(8,128)(2,1)S(1)}, u32[]{:S(2)}, u32[]{:S(2)}) collective-permute-start(bf16[128,5120]{0,1:T(8,128)(2,1)S(1)} %pad_maximum_fusion.4), channel_id=1, source_target_pairs={{0,16},{16,0},{1,17},{17,1},{2,18},{18,2},{3,19},{19,3},{4,20},{20... | collective-permute-start | bytes 3932168 | tf_op jit(solution)/shard_map/ppermute | solution.py:18
  435.3 34.2 %collective-permute-start.55 = (bf16[512,1280]{0,1:T(8,128)(2,1)}, bf16[512,1280]{0,1:T(8,128)(2,1)}, u32[]{:S(2)}, u32[]{:S(2)}) collective-permute-start(bf16[512,1280]{0,1:T(8,128)(2,1)} %pad_maximum_fusion.8), channel_id=1, source_target_pairs={{0,16},{16,0},{1,17},{17,1},{2,18},{18,2},{3,19},{19,3},{4,20},{20... | collective-permute-start | bytes 3932168 | tf_op jit(solution)/shard_map/ppermute | solution.py:18
  441.8 144.5 %collective-permute-start.78 = (bf16[1024,1024]{1,0:T(8,128)(2,1)}, bf16[1024,1024]{1,0:T(8,128)(2,1)}, u32[]{:S(2)}, u32[]{:S(2)}) collective-permute-start(bf16[1024,1024]{1,0:T(8,128)(2,1)} %convolution_convert_fusion.2), channel_id=1, source_target_pairs={{0,16},{1,17},{2,18},{3,19},{4,20},{5,21},{6,22},{7,23},{8,24},{9,... | collective-permute-start | bytes 6291464 | tf_op jit(solution)/shard_map/ppermute | solution.py:278
  482.0 130.6 %collective-permute-start.87 = (f32[1024]{0:T(1024)S(1)}, f32[1024]{0:T(1024)S(1)}, u32[]{:S(2)}, u32[]{:S(2)}) collective-permute-start(f32[1024]{0:T(1024)S(1)} %add_add_fusion), channel_id=1, source_target_pairs={{0,16},{1,17},{2,18},{3,19},{4,20},{5,21},{6,22},{7,23},{8,24},{9,... | collective-permute-start | bytes 12296 | tf_op jit(solution)/shard_map/ppermute | solution.py:278
  517.7 29.0 %collective-permute-start.44 = (bf16[128,1280]{1,0:T(8,128)(2,1)S(1)}, bf16[128,1280]{1,0:T(8,128)(2,1)}, u32[]{:S(2)}, u32[]{:S(2)}) collective-permute-start(bf16[128,1280]{1,0:T(8,128)(2,1)S(1)} %fusion.24), channel_id=1, source_target_pairs={{0,3},{1,0},{2,1},{3,2},{4,7},{5,4},{6,5},{7,6},{8,11},{9,8},{10,9... | collective-permute-start | bytes 983048 | tf_op jit(solution)/shard_map/ppermute | solution.py:18
  568.6 57.5 %collective-permute-start.59 = (bf16[1280,1024]{1,0:T(8,128)(2,1)}, bf16[1280,1024]{1,0:T(8,128)(2,1)}, u32[]{:S(2)}, u32[]{:S(2)}) collective-permute-start(bf16[1280,1024]{1,0:T(8,128)(2,1)} %convolution_convert_fusion), channel_id=1, source_target_pairs={{0,16},{1,17},{2,18},{3,19},{4,20},{5,21},{6,22},{7,23},{8,24},{9,... | collective-permute-start | bytes 7864328 | tf_op jit(solution)/shard_map/ppermute | solution.py:278
  582.7 30.9 %collective-permute-start.79 = (bf16[1024,1024]{1,0:T(8,128)(2,1)}, bf16[1024,1024]{1,0:T(8,128)(2,1)}, u32[]{:S(2)}, u32[]{:S(2)}) collective-permute-start(bf16[1024,1024]{1,0:T(8,128)(2,1)} %convolution_convert_fusion.3), channel_id=1, source_target_pairs={{16,0},{17,1},{18,2},{19,3},{20,4},{21,5},{22,6},{23,7},{24,8},{25... | collective-permute-start | bytes 6291464 | tf_op jit(solution)/shard_map/ppermute | solution.py:279
  595.5 32.6 %collective-permute-start.60 = (bf16[1280,1024]{1,0:T(8,128)(2,1)}, bf16[1280,1024]{1,0:T(8,128)(2,1)}, u32[]{:S(2)}, u32[]{:S(2)}) collective-permute-start(bf16[1280,1024]{1,0:T(8,128)(2,1)} %convolution_convert_fusion.1), channel_id=1, source_target_pairs={{16,0},{17,1},{18,2},{19,3},{20,4},{21,5},{22,6},{23,7},{24,8},{25... | collective-permute-start | bytes 7864328 | tf_op jit(solution)/shard_map/ppermute | solution.py:279
  (138 other events, 1663.6 us)
where the time goes:
time: 660 us; the launch traced here: 650 us
  waiting for transfers between devices  239 us (36%)
  local copies, waits for them, and re-layouts  129 us (20%)
  starting transfers between devices  107 us (16%)
  other arithmetic  87.5 us (13%)
  matrix products  83.9 us (13%)
    ppermute x83, waiting for transfers between devices, shifted(): lax.ppermute(value, axis, [(i, (i + steps) % count) for i in range(count)])  239 us
    ppermute x83, starting transfers between devices, shifted(): lax.ppermute(value, axis, [(i, (i + steps) % count) for i in range(count)])  94.4 us
    unnamed x190, local copies, waits for them, and re-layouts  84.7 us
    dot_general x4, matrix products, contract_cols(): lax.dot_general(first, second, (((1,), (1,)), ((), ())), preferred_elemen...  37.6 us
    select_n x2, other arithmetic, halves(): kept = jnp.where(sec == 0, first, second)  22 us
    dot_general x4, matrix products, contract_rows(): lax.dot_general(first, second, (((0,), (0,)), ((), ())), preferred_elemen...  19.1 us
    concatenate x3, other arithmetic, pair(): return jnp.concatenate([value, swap(value)])  14.4 us
  transfers between devices with their start and end apart: 89, of which 32 were waited for; matrix products, arithmetic and copies ran while one was open for 34% of the time, Pallas kernels for 0%

commit v1 on v0

v1 whole, which is shorter than its diff:
```python
import jax
import jax.numpy as jnp
from jax import lax
from jax.experimental import pallas as pl
from jax.experimental.pallas import tpu as pltpu
from jax.sharding import PartitionSpec as P

HD = 128

eps = 1e-06
adv_step = 0.0625
masked_score = -1e30

f32 = jnp.float32
bf16 = jnp.bfloat16


def shifted(value, axis, steps):
    count = lax.axis_size(axis)
    return lax.ppermute(value, axis, [(i, (i + steps) % count) for i in range(count)])


def swap(value):
    return shifted(value, "section", 1)


def gathered_list(value, axis):
    return [value] + [shifted(value, axis, d) for d in range(1, lax.axis_size(axis))]


def messages(chunk_of, axis):
    count = lax.axis_size(axis)
    me = lax.axis_index(axis)
    return [chunk_of(lax.rem(me + d, count)) for d in range(count)]


def delivered(pieces, axis):
    return [pieces[0]] + [shifted(pieces[d], axis, d) for d in range(1, len(pieces))]


def after(value, *others):
    return lax.optimization_barrier((value, others))[0]


def small_sum(value, axis):
    total = value
    for piece in gathered_list(value, axis)[1:]:
        total = total + piece
    return total


def contract_rows(first, second):
    return lax.dot_general(first, second, (((0,), (0,)), ((), ())), preferred_element_type=f32)


def contract_cols(first, second):
    return lax.dot_general(first, second, (((1,), (1,)), ((), ())), preferred_element_type=f32)


VMEM_BYTES = 44 * 1024 * 1024


def params():
    return pltpu.CompilerParams(vmem_limit_bytes=VMEM_BYTES)


def small_cost():
    return pl.CostEstimate(flops=0, bytes_accessed=1024, transcendentals=0)


def diagonal(count):
    return lax.broadcasted_iota(jnp.int32, (count, count), 0) == lax.broadcasted_iota(
        jnp.int32, (count, count), 1
    )


def as_column(row):
    return jnp.sum(jnp.where(diagonal(row.shape[1]), row, 0.0), axis=1, keepdims=True)


def as_row(column):
    return jnp.sum(jnp.where(diagonal(column.shape[0]), column, 0.0), axis=0, keepdims=True)


def whole(shape):
    return pl.BlockSpec(shape, lambda *_: (0,) * len(shape))


ANY = pl.BlockSpec(memory_space=pl.ANY)


def start_copies(flags_ref, split_ref, got_ref, copies):
    section = flags_ref[1]

    @pl.when(flags_ref[0] == 1)
    def _():
        for start, size, target, sem in copies:
            pltpu.make_async_copy(
                split_ref.at[section, pl.ds(start, size)], target, sem
            ).start()

    @pl.when(flags_ref[0] == 0)
    def _():
        for start, size, target, sem in copies:
            pltpu.make_async_copy(got_ref.at[pl.ds(start, size)], target, sem).start()

    return [
        pltpu.make_async_copy(got_ref.at[pl.ds(start, size)], target, sem)
        for start, size, target, sem in copies
    ]


def project(value, weights, flags, parts, chunks):
    both, feat = value.shape
    own = both // 2
    cols = sum(size for size, _ in parts)
    pieces = [(chunk, *part) for chunk in range(chunks) for part in parts]

    def kernel(flags_ref, value_ref, split_ref, got_ref, own_ref, other_ref, held, sems):
        copies = []
        start = 0
        for number, (chunk, size, first_row) in enumerate(pieces):
            copies.append(
                (first_row(chunk), size, held.at[pl.ds(start, size)], sems.at[number])
            )
            start += size
        waits = start_copies(flags_ref, split_ref, got_ref, copies)
        for chunk in range(chunks):
            for wait in waits[chunk * len(parts) : (chunk + 1) * len(parts)]:
                wait.wait()
            product = contract_cols(
                value_ref[...], held[chunk * cols : (chunk + 1) * cols, :]
            ).astype(bf16)
            own_ref[chunk] = product[:own]
            other_ref[chunk] = product[own:]

    out = jax.ShapeDtypeStruct((chunks, own, cols), bf16)
    return pl.pallas_call(
        kernel,
        grid_spec=pltpu.PrefetchScalarGridSpec(
            num_scalar_prefetch=1,
            grid=(1,),
            in_specs=[whole((both, feat)), ANY, ANY],
            out_specs=[whole(out.shape)] * 2,
            scratch_shapes=[
                pltpu.VMEM((chunks * cols, feat), bf16),
                pltpu.SemaphoreType.DMA((len(pieces),)),
            ],
        ),
        out_shape=[out] * 2,
        compiler_params=params(),
        cost_estimate=small_cost(),
        name="project",
    )(flags, value, *weights)


def combine(own_pieces, other_pieces, weights, flags, parts, extras, finish, out_shape):
    chunks, own, cols = own_pieces.shape
    feat = weights[1].shape[-1]
    count = len(parts)

    def kernel(flags_ref, own_ref, other_ref, split_ref, got_ref, *refs):
        extra_refs = refs[: len(extras)]
        outs = refs[len(extras) : -3]
        held, sems, total = refs[-3:]
        copies = []
        for step in range(chunks):
            start = step * cols
            for part, (size, first_row) in enumerate(parts):
                row = pl.multiple_of(first_row(flags_ref[2 + step]), HD)
                copies.append(
                    (row, size, held.at[pl.ds(start, size)], sems.at[step * count + part])
                )
                start += size
        waits = start_copies(flags_ref, split_ref, got_ref, copies)
        for step in range(chunks):
            for wait in waits[step * count : (step + 1) * count]:
                wait.wait()
            left = jnp.concatenate([own_ref[step], other_ref[step]], axis=0)
            product = jnp.dot(
                left, held[step * cols : (step + 1) * cols, :], preferred_element_type=f32
            )
            if step == 0:
                total[...] = product
            else:
                total[...] += product
        finish(total, extra_refs, outs)

    return pl.pallas_call(
        kernel,
        grid_spec=pltpu.PrefetchScalarGridSpec(
            num_scalar_prefetch=1,
            grid=(1,),
            in_specs=[whole(own_pieces.shape)] * 2
            + [ANY, ANY]
            + [whole(extra.shape) for extra in extras],
            out_specs=[whole(shape.shape) for shape in out_shape],
            scratch_shapes=[
                pltpu.VMEM((chunks * cols, feat), bf16),
                pltpu.SemaphoreType.DMA((chunks * count,)),
                pltpu.VMEM((2 * own, feat), f32),
            ],
        ),
        out_shape=out_shape,
        compiler_params=params(),
        cost_estimate=small_cost(),
        name="combine",
    )(flags, own_pieces, other_pieces, *weights, *extras)


def regroup(pieces, table, count):
    own = pieces.shape[1]
    heads = table.shape[1] // count

    def kernel(table_ref, pieces_ref, out_ref):
        for block in range(count):
            for head in range(heads):
                place = block * heads + head
                column = pl.multiple_of(table_ref[1, place], HD)
                out_ref[block, :, head * HD : (head + 1) * HD] = pieces_ref[
                    table_ref[0, place], :, pl.ds(column, HD)
                ]

    out = jax.ShapeDtypeStruct((count, own, heads * HD), pieces.dtype)
    return pl.pallas_call(
        kernel,
        grid_spec=pltpu.PrefetchScalarGridSpec(
            num_scalar_prefetch=1,
            grid=(1,),
            in_specs=[whole(pieces.shape)],
            out_specs=whole(out.shape),
        ),
        out_shape=out,
        compiler_params=params(),
        cost_estimate=small_cost(),
        name="regroup",
    )(table, pieces)


def outer(own_left, other_left, right, order):
    groups, own, block = own_left.shape
    feat = right.shape[-1]
    tokens = groups * own
    step = 256 if block % 256 == 0 else block

    def kernel(order_ref, own_ref, other_ref, right_ref, out_ref, left, held):
        for d in range(groups):
            here = slice(d * own, (d + 1) * own)
            there = slice(tokens + d * own, tokens + (d + 1) * own)
            left[here] = own_ref[d]
            left[there] = other_ref[d]
            held[here] = right_ref[order_ref[d], :own, :]
            held[there] = right_ref[order_ref[d], own:, :]
        for start in range(0, block, step):
            out_ref[start : start + step, :] = contract_rows(
                left[:, start : start + step], held[...]
            ).astype(bf16)

    return pl.pallas_call(
        kernel,
        grid_spec=pltpu.PrefetchScalarGridSpec(
            num_scalar_prefetch=1,
            grid=(1,),
            in_specs=[whole(own_left.shape)] * 2 + [whole(right.shape)],
            out_specs=whole((block, feat)),
            scratch_shapes=[
                pltpu.VMEM((2 * tokens, block), bf16),
                pltpu.VMEM((2 * tokens, feat), bf16),
            ],
        ),
        out_shape=jax.ShapeDtypeStruct((block, feat), bf16),
        compiler_params=params(),
        cost_estimate=small_cost(),
        name="outer",
    )(order, own_left, other_left, right)


def interleave(layer_0, layer_1, first_got, second_got, flags):
    count, feat = layer_0.shape
    step = 256 if count % 256 == 0 else count

    def kernel(flags_ref, layer_0_ref, layer_1_ref, first_ref, second_ref, out_ref):
        @pl.when(flags_ref[1] == 0)
        def _():
            out_ref[...] = jnp.stack([layer_0_ref[...], second_ref[...]], axis=1)

        @pl.when(flags_ref[1] == 1)
        def _():
            out_ref[...] = jnp.stack([first_ref[...], layer_1_ref[...]], axis=1)

    in_first = pl.BlockSpec((step, feat), lambda i, f: (i * (1 - f[1]), 0))
    in_second = pl.BlockSpec((step, feat), lambda i, f: (i * f[1], 0))
    return pl.pallas_call(
        kernel,
        grid_spec=pltpu.PrefetchScalarGridSpec(
            num_scalar_prefetch=1,
            grid=(count // step,),
            in_specs=[in_first, in_second, in_second, in_first],
            out_specs=pl.BlockSpec((step, 2, feat), lambda i, f: (i, 0, 0)),
        ),
        out_shape=jax.ShapeDtypeStruct((count, 2, feat), bf16),
        compiler_params=params(),
        cost_estimate=small_cost(),
        name="interleave",
    )(flags, layer_0, layer_1, first_got, second_got)


def attend(pieces, square, lens, width, heads, kv_local):
    own, cols = pieces[0].shape
    count, per = len(pieces), lens.shape[0]
    length = own // per
    per_share = heads // kv_local
    q_cols = heads * HD

    def kernel(lens_ref, *refs):
        piece_refs, square_ref = refs[:count], refs[count]
        linear_ref, scaled_ref, prob_ref, inv_ref, out_ref = refs[count + 1 :]
        linear = piece_refs[0][...].astype(f32)
        for ref in piece_refs[1:]:
            linear = linear + ref[...].astype(f32)
        linear_ref[...] = linear
        inv = lax.rsqrt(square_ref[...] / width + eps)
        inv_ref[...] = inv
        scaled_ref[...] = (as_column(inv) * linear).astype(bf16)
        rows = lax.broadcasted_iota(jnp.int32, (length, length), 0)
        columns = lax.broadcasted_iota(jnp.int32, (length, length), 1)
        for slot in range(per):
            here = slice(slot * length, (slot + 1) * length)
            mask = (columns <= rows) & (columns < lens_ref[slot])
            for head in range(heads):
                share = head // per_share
                queries = scaled_ref[here, head * HD : (head + 1) * HD]
                keys = scaled_ref[here, q_cols + share * HD : q_cols + (share + 1) * HD]
                start = q_cols + (kv_local + share) * HD
                values = scaled_ref[here, start : start + HD]
                scores = contract_cols(queries, keys) * HD ** (-0.5)
                scores = jnp.where(mask, scores, masked_score)
                terms = jnp.exp(scores - jnp.max(scores, axis=-1, keepdims=True))
                terms = jnp.where(mask, terms, 0.0)
                attention = terms / jnp.sum(terms, axis=-1, keepdims=True)
                prob_ref[slot * heads + head] = attention
                out_ref[here, head * HD : (head + 1) * HD] = jnp.dot(
                    attention.astype(bf16), values, preferred_element_type=f32
                ).astype(bf16)

    outs = [
        jax.ShapeDtypeStruct((own, cols), f32),
        jax.ShapeDtypeStruct((own, cols), bf16),
        jax.ShapeDtypeStruct((per * heads, length, length), f32),
        jax.ShapeDtypeStruct((1, own), f32),
        jax.ShapeDtypeStruct((own, q_cols), bf16),
    ]
    return pl.pallas_call(
        kernel,
        grid_spec=pltpu.PrefetchScalarGridSpec(
            num_scalar_prefetch=1,
            grid=(1,),
            in_specs=[whole((own, cols))] * count + [whole((1, own))],
            out_specs=[whole(shape.shape) for shape in outs],
        ),
        out_shape=outs,
        compiler_params=params(),
        cost_estimate=small_cost(),
        name="attend",
    )(lens, *pieces, square)


def attend_back(pieces, linear, scaled, prob, inv, heads, kv_local):
    own, cols = linear.shape
    count = len(pieces)
    length = prob.shape[1]
    per = own // length
    per_share = heads // kv_local
    q_cols = heads * HD

    def kernel(*refs):
        piece_refs = refs[:count]
        linear_ref, scaled_ref, prob_ref, inv_ref, low_ref, scale_ref = refs[count:]
        inv_column = as_column(inv_ref[...])
        total = piece_refs[0][...].astype(f32)
        for ref in piece_refs[1:]:
            total = total + ref[...].astype(f32)
        grads_all = total.astype(bf16)
        for slot in range(per):
            here = slice(slot * length, (slot + 1) * length)
            inv_here = inv_column[here]
            scale_sum = jnp.zeros((length, 1), f32)

            def emit(part, start, scale_sum):
                low_ref[here, start : start + HD] = (inv_here * part).astype(bf16)
                return scale_sum + jnp.sum(
                    part * linear_ref[here, start : start + HD], axis=1, keepdims=True
                )

            for share in range(kv_local):
                key_start = q_cols + share * HD
                value_start = q_cols + (kv_local + share) * HD
                keys = scaled_ref[here, key_start : key_start + HD]
                values = scaled_ref[here, value_start : value_start + HD]
                key_sum = jnp.zeros((length, HD), f32)
                value_sum = jnp.zeros((length, HD), f32)
                for member in range(per_share):
                    head = share * per_share + member
                    queries = scaled_ref[here, head * HD : (head + 1) * HD]
                    grads = grads_all[here, head * HD : (head + 1) * HD]
                    attention = prob_ref[slot * heads + head]
                    d_prob = contract_cols(grads, values)
                    mean = jnp.sum(attention * d_prob, axis=-1, keepdims=True)
                    d_score = (attention * (d_prob - mean) * HD ** (-0.5)).astype(bf16)
                    d_query = jnp.dot(d_score, keys, preferred_element_type=f32)
                    scale_sum = emit(d_query.astype(bf16).astype(f32), head * HD, scale_sum)
                    key_sum = key_sum + contract_rows(d_score, queries).astype(bf16).astype(f32)
                    value_sum = value_sum + contract_rows(attention.astype(bf16), grads).astype(
                        bf16
                    ).astype(f32)
                scale_sum = emit(key_sum, key_start, scale_sum)
                scale_sum = emit(value_sum, value_start, scale_sum)
            scale_ref[:, here] = as_row(scale_sum)

    outs = [jax.ShapeDtypeStruct((own, cols), bf16), jax.ShapeDtypeStruct((1, own), f32)]
    return pl.pallas_call(
        kernel,
        grid=(1,),
        in_specs=[whole((own, q_cols))] * count
        + [whole(value.shape) for value in (linear, scaled, prob, inv)],
        out_specs=[whole(shape.shape) for shape in outs],
        out_shape=outs,
        compiler_params=params(),
        cost_estimate=small_cost(),
        name="attend_back",
    )(*pieces, linear, scaled, prob, inv)


def shards(hidden, head_grad, w_in, w_out, gain, dest_slot, lengths, advantage):
    sections = lax.axis_size("section")
    groups = lax.axis_size("dp")
    tensors = lax.axis_size("tensor")
    sec = lax.axis_index("section")
    grp = lax.axis_index("dp")
    ten = lax.axis_index("tensor")
    assert sections == 2
    rows, length, feat = hidden.shape[0], hidden.shape[1], hidden.shape[4]
    width = sections * tensors * feat
    qkv_width = w_in.shape[1]
    out_width = w_out.shape[1]
    total_heads = out_width // HD
    kv_total = (qkv_width - out_width) // (2 * HD)
    group_size = total_heads // kv_total
    heads = total_heads // tensors
    kv_local = max(1, heads // group_size)
    sharers = tensors * kv_local // kv_total
    q_cols, kv_cols = heads * HD, kv_local * HD
    per = rows // sections
    own, both = per * length, rows * length
    in_rows, out_rows = qkv_width // groups, out_width // groups

    order = jnp.concatenate(
        [sec * per + jnp.arange(per), (1 - sec) * per + jnp.arange(per)]
    ).astype(jnp.int32)
    slot_ids = grp * rows + order
    matches = dest_slot[None, :] == slot_ids[:, None]
    slot_live = jnp.any(matches, axis=1)
    slot_len = jnp.maximum(jnp.sum(jnp.where(matches, lengths[None, :], 0), axis=1), 1)
    slot_adv = jnp.sum(jnp.where(matches[:, :, None], advantage[None, :, :], 0), axis=1)
    positions = jnp.arange(length, dtype=jnp.int32)

    def own_first(value):
        return jnp.concatenate(
            [
                lax.dynamic_slice_in_dim(value, sec * per, per),
                lax.dynamic_slice_in_dim(value, (1 - sec) * per, per),
            ]
        )

    sent_rows = own_first(hidden.reshape(rows, length, feat))
    w_in = after(w_in, sent_rows)
    blocks = gathered_list(sent_rows, "dp")
    routed = jnp.zeros((rows, length, feat), bf16)
    for d, block in enumerate(blocks):
        source = lax.rem(grp + groups - d, groups)
        hit = dest_slot[source * rows + order] == slot_ids
        routed = jnp.where(hit[:, None, None], block, routed)
    entry = routed.reshape(both, feat)

    def split_halves(weights):
        return weights.reshape(weights.shape[1], sections, feat).transpose(1, 0, 2)

    def half(split, index):
        return lax.dynamic_index_in_dim(split, index, 0, keepdims=False)

    win_split = lax.optimization_barrier(split_halves(w_in))
    win_sent = half(win_split, 1 - sec)
    win = win_split, swap(win_sent)
    wout_split = lax.optimization_barrier(split_halves(after(w_out, win_sent)))
    wout_sent = half(wout_split, 1 - sec)
    wout = wout_split, swap(wout_sent)
    gain_rows = gain.reshape(sections, 1, feat)
    gain_kept = lax.dynamic_index_in_dim(gain_rows, sec, 0, keepdims=False)
    gain_got = swap(lax.dynamic_index_in_dim(gain_rows, 1 - sec, 0, keepdims=False))

    def gain_of(layer):
        return jnp.where(sec == layer, gain_kept, gain_got)

    from_chunk = jnp.arange(tensors)

    def flags_of(layer):
        head = jnp.stack([(sec == layer).astype(jnp.int32), sec.astype(jnp.int32)])
        return jnp.concatenate([head, from_chunk.astype(jnp.int32)])

    def kv_row(index):
        return lax.div(index * heads, group_size) * HD

    out_parts = [(q_cols, lambda index: index * q_cols)]
    in_parts = out_parts + [
        (kv_cols, lambda index: out_width + kv_row(index)),
        (kv_cols, lambda index: out_width + kv_total * HD + kv_row(index)),
    ]

    token_keep = (positions[None, :] < slot_len[:, None]) & slot_live[:, None]
    factor = jnp.where(token_keep, slot_adv.astype(f32) * adv_step, 0.0)
    grad_half = lax.dynamic_index_in_dim(
        head_grad.reshape(rows, length, sections, feat), sec, 2, keepdims=False
    )
    seed = (own_first(grad_half).astype(f32) * factor[:, :, None]).astype(bf16).reshape(both, feat)
    own_len = slot_len[:per]

    def head_sum(own_products, other_products):
        total = own_products.astype(f32) + swap(other_products).astype(f32)
        return lax.psum_scatter(total.astype(bf16), "tensor", scatter_dimension=0)

    def forward_attention(normed, square, summed):
        square = small_sum(square[:, :own] + swap(square[:, own:]), "tensor")
        linear, scaled, prob, inv, attended = attend(
            [summed], square, own_len, width, heads, kv_local
        )
        return normed, linear, scaled, prob, inv, attended

    def gathered_heads(value, *others):
        return after(lax.all_gather(value, "tensor"), *others)

    def backward_attention(own_grad, saved):
        normed, linear, scaled, prob, inv, _ = saved
        low, d_scale = attend_back([own_grad], linear, scaled, prob, inv, heads, kv_local)
        d_scale = small_sum(d_scale, "tensor")
        coefficient = d_scale * inv**3 * (-1.0 / width)
        return low, jnp.concatenate([coefficient, swap(coefficient)], axis=1)

    def in_columns(pieces, start, size):
        return pieces[:, :, start : start + size].transpose(1, 0, 2).reshape(own, tensors * size)

    def kv_columns(pieces, start):
        part = in_columns(pieces, start, kv_cols)
        if sharers > 1:
            part = part.reshape(own, kv_total, sharers, HD).astype(f32)
            part = jnp.sum(part, axis=2).astype(bf16).reshape(own, kv_total * HD)
        return part

    def all_columns(pieces):
        return jnp.concatenate(
            [
                in_columns(pieces, 0, q_cols),
                kv_columns(pieces, q_cols),
                kv_columns(pieces, q_cols + kv_cols),
            ],
            axis=1,
        )

    def pair(value):
        return jnp.concatenate([value, swap(value)])

    to_group = (grp + jnp.arange(groups)) % groups

    def head_table(chunks, columns):
        table = jnp.stack([chunks, columns]).reshape(2, groups, -1)
        return jnp.take(table, to_group, axis=1).reshape(2, -1).astype(jnp.int32)

    every_head = jnp.arange(total_heads)
    every_share = jnp.arange(kv_total)
    out_table = head_table(every_head // heads, every_head % heads * HD)
    in_table = head_table(
        jnp.concatenate([every_head // heads] + [every_share // kv_local] * 2),
        jnp.concatenate(
            [
                every_head % heads * HD,
                q_cols + every_share % kv_local * HD,
                q_cols + kv_cols + every_share % kv_local * HD,
            ]
        ),
    )

    def in_blocks(low_pieces):
        if sharers == 1:
            return regroup(low_pieces, in_table, groups)
        blocks = all_columns(low_pieces).reshape(own, groups, in_rows)
        return jnp.take(blocks.transpose(1, 0, 2), to_group, axis=0)

    def lefts(pieces):
        stacked = jnp.stack(pieces)
        return stacked, swap(stacked)

    def of_groups(value):
        return jnp.stack(gathered_list(value, "dp"))

    def weight_grad(left, right):
        return outer(*left, right, jnp.arange(groups, dtype=jnp.int32))

    states = entry.astype(f32)
    normed_0 = (states * gain_of(0)).astype(bf16)
    square_0 = jnp.sum(states * states, axis=1)[None]
    summed_0 = head_sum(*project(normed_0, win, flags_of(0), in_parts, tensors))
    normed_all_0 = of_groups(normed_0)
    saved_0 = forward_attention(normed_0, square_0, after(summed_0, normed_all_0))
    seed_products = project(seed, wout, flags_of(1), out_parts, tensors)
    seed_all = of_groups(seed)
    heads_0 = gathered_heads(saved_0[-1], seed_all)
    seed_grad = head_sum(*after(seed_products, heads_0))

    def next_layer(total, extras, outs):
        hidden_ref, gain_ref = extras
        hidden_out, normed_out, square_out = outs
        value = (hidden_ref[...].astype(f32) + total[...]).astype(bf16)
        hidden_out[...] = value
        value = value.astype(f32)
        normed_out[...] = (value * gain_ref[...]).astype(bf16)
        square_out[...] = as_row(jnp.sum(value * value, axis=1, keepdims=True))

    activation = jax.ShapeDtypeStruct((both, feat), bf16)
    hidden_1, normed_1, square_1 = combine(
        heads_0,
        swap(heads_0),
        wout,
        flags_of(0),
        out_parts,
        [entry, gain_of(1)],
        next_layer,
        [activation, activation, jax.ShapeDtypeStruct((1, both), f32)],
    )
    summed_1 = head_sum(*project(normed_1, win, flags_of(1), in_parts, tensors))
    out_sent_0 = delivered(list(regroup(heads_0, out_table, groups)), "dp")
    out_left_0 = lefts(out_sent_0)
    saved_1 = forward_attention(normed_1, square_1, after(summed_1, out_left_0))
    normed_all_1 = of_groups(normed_1)

    def previous_layer(total, extras, outs):
        grad_ref, hidden_ref, gain_ref, coefficient_ref = extras
        grad_out, gain_out = outs
        states = hidden_ref[...].astype(f32)
        grad_out[...] = (
            grad_ref[...].astype(f32)
            + total[...] * gain_ref[...]
            + as_column(coefficient_ref[...]) * states
        ).astype(bf16)
        gain_out[...] = jnp.sum(total[...] * states, axis=0, keepdims=True)

    def input_grad(grad, hidden_in, low_pieces, coefficient, layer):
        return combine(
            low_pieces,
            swap(low_pieces),
            win,
            flags_of(layer),
            in_parts,
            [grad, hidden_in, gain_of(layer), coefficient],
            previous_layer,
            [activation, jax.ShapeDtypeStruct((1, feat), f32)],
        )

    def shaped(layer_0, layer_1, count):
        first_got = lax.ppermute(layer_1, "section", [(0, 1)])
        second_got = lax.ppermute(layer_0, "section", [(1, 0)])
        joined = interleave(layer_0, layer_1, first_got, second_got, flags_of(0))
        return joined.reshape(1, count, sections, 1, feat)

    low, coefficient_1 = backward_attention(seed_grad, saved_1)
    low_1 = gathered_heads(low, normed_all_1)
    heads_1 = gathered_heads(after(saved_1[-1], low))
    grad_1, gain_1 = input_grad(seed, hidden_1, low_1, coefficient_1, 1)
    own_grad = head_sum(*project(grad_1, wout, flags_of(0), out_parts, tensors))
    in_sent_1 = delivered(list(in_blocks(low_1)), "dp")
    out_sent_1 = delivered(list(regroup(heads_1, out_table, groups)), "dp")
    own_grad = after(own_grad, in_sent_1, out_sent_1)
    grad_all = of_groups(grad_1)

    low, coefficient_0 = backward_attention(own_grad, saved_0)
    in_1 = weight_grad(lefts(in_sent_1), normed_all_1)
    out_1 = weight_grad(lefts(out_sent_1), seed_all)
    out_0 = weight_grad(out_left_0, grad_all)
    low_0 = gathered_heads(low, in_1, out_1, out_0)
    blocks = in_blocks(low_0)
    low_0 = after(low_0, blocks)
    _, gain_0 = input_grad(grad_1, entry, low_0, coefficient_0, 0)
    grad_out = shaped(after(out_0, blocks), out_1, out_rows)
    in_sent_0 = delivered(list(blocks), "dp")
    in_0 = weight_grad(lefts(after(in_sent_0, gain_0, grad_out)), normed_all_0)

    gains = jnp.concatenate([gain_0, gain_1])
    gains = small_sum(gains, "dp")
    kept = lax.dynamic_index_in_dim(gains, sec, 0, keepdims=False)
    got = swap(lax.dynamic_index_in_dim(gains, 1 - sec, 0, keepdims=False))
    grad_gain = jnp.stack([jnp.where(sec == 0, kept, got), jnp.where(sec == 0, got, kept)])
    grad_gain = grad_gain.reshape(1, sections, 1, feat)
    return (shaped(in_0, in_1, in_rows), grad_out, grad_gain)


def solution(mesh):
    placed = (
        P("dp", None, "section", "tensor", None),
        P("dp", None, None, "tensor", None),
        P("section", None, None, "tensor", None),
        P("section", None, None, "tensor", None),
        P("section", None, "tensor", None),
        P(),
        P(),
        P(),
    )
    return jax.shard_map(
        shards,
        mesh=mesh,
        in_specs=placed,
        out_specs=(
            P("section", "dp", None, "tensor", None),
            P("section", "dp", None, "tensor", None),
            P("section", None, "tensor", None),
        ),
        check_vma=False,
    )
```

time: 660 us -> 478 us (0.72)
  the two profiles are of different devices: /device:TPU:11 before, /device:TPU:0 now
where the time goes in v1:
time: 478 us; the launch traced here: 468 us
  waiting for transfers between devices  188 us (39%)
  local copies, waits for them, and re-layouts  90.4 us (19%)
  Pallas kernels  87.8 us (18%)
  starting transfers between devices  70.4 us (15%)
  other arithmetic  16.9 us (4%)
  between operations  15.1 us (3%)
    ppermute x61, waiting for transfers between devices, shifted(): lax.ppermute(value, axis, [(i, (i + steps) % count) for i in range(count)])  171 us
    ppermute x61, starting transfers between devices, shifted(): lax.ppermute(value, axis, [(i, (i + steps) % count) for i in range(count)])  60.3 us
    optimization_barrier x2, local copies, waits for them, and re-layouts, after(): return lax.optimization_barrier((value, others))[0]  36.9 us
    unnamed x94, local copies, waits for them, and re-layouts  27.5 us
    pallas_call x4, Pallas kernels, project(): pl.pallas_call(kernel, grid_spec=pltpu.PrefetchScalarGridSpec(num_scalar_...  23.1 us
    pallas_call x3, Pallas kernels, combine(): pl.pallas_call(kernel, grid_spec=pltpu.PrefetchScalarGridSpec(num_scalar_...  18.3 us
    pallas_call x2, Pallas kernels, interleave(): pl.pallas_call(kernel, grid_spec=pltpu.PrefetchScalarGridSpec(num_scalar_...  17.5 us
    squeeze x2, local copies, waits for them, and re-layouts, half(): return lax.dynamic_index_in_dim(split, index, 0, keepdims=False)  16.9 us
  transfers between devices with their start and end apart: 73, of which 42 were waited for; matrix products, arithmetic and copies ran while one was open for 10% of the time, Pallas kernels for 13%

profile of v1, /device:TPU:0, one launch (start us, length us, event | category | flops | bytes accessed | tf_op | source)
XLA Modules:
  0.0 468.4 jit_solution(14033075363160019660)
XLA Ops:
  8.3 20.5 %copy.41 = bf16[1,5120,2,1,1024]{4,1,2,3,0:T(8,128)(2,1)} copy(bf16[1,5120,2,1,1024]{4,2,3,1,0:T(2,128)(2,1)} %param.10) | data formatting | bytes 41943040 | tf_op jit(solution)/shard_map/optimization_barrier | solution.py:42
  28.8 9.2 %dynamic-slice_bitcast_fusion = bf16[5120,1024]{1,0:T(8,128)(2,1)} fusion(bf16[2,5120,1024]{2,1,0:T(8,128)(2,1)} %bitcast.161, s32[]{:T(128)S(6)} %select_n.222), kind=kLoop, calls=%fused_computation.8 | loop fusion | bytes 20971524 | tf_op jit(solution)/shard_map/jit(dynamic_index_in_dim)/squeeze | solution.py:489
  42.4 16.4 %copy.42 = bf16[1,4096,2,1,1024]{4,1,2,3,0:T(8,128)(2,1)} copy(bf16[1,4096,2,1,1024]{4,2,3,1,0:T(2,128)(2,1)} %param.11) | data formatting | bytes 33554432 | tf_op jit(solution)/shard_map/optimization_barrier | solution.py:42
  58.8 7.7 %dynamic-slice_bitcast_fusion.1 = bf16[4096,1024]{1,0:T(8,128)(2,1)} fusion(bf16[2,4096,1024]{2,1,0:T(8,128)(2,1)} %bitcast.166, s32[]{:T(128)S(6)} %select_n.222), kind=kLoop, calls=%fused_computation.9 | loop fusion | bytes 16777220 | tf_op jit(solution)/shard_map/jit(dynamic_index_in_dim)/squeeze | solution.py:489
  73.2 14.4 %collective-permute-done.3 = bf16[2,128,1024]{2,1,0:T(8,128)(2,1)S(1)} collective-permute-done((bf16[2,128,1024]{2,1,0:T(8,128)(2,1)S(1)}, bf16[2,128,1024]{2,1,0:T(8,128)(2,1)S(1)}, u32[]{:S(2)}, u32[]{:S(2)}) %collective-permute-start.3) | collective-permute-done | bytes 524320 | tf_op jit(solution)/shard_map/ppermute | solution.py:20
  88.2 6.4 %project.5 = (bf16[4,128,1280]{2,1,0:T(8,128)(2,1)S(1)}, bf16[4,128,1280]{2,1,0:T(8,128)(2,1)S(1)}) custom-call(s32[6]{0:T(128)S(1)} %get-tuple-element.143.flags_ref, bf16[256,1024]{1,0:T(8,128)(2,1)S(1)} %multiply_convert_fusion.value_ref, bf16[2,5120,1024]{2,1,0:T(8,128)(2,1)} %bitcast.162, bf16[5120,1024]{1,0:T(8,128)(2,1)} %collective-permute-done.5.got_ref), custom_call_target="tpu_custom_call" | custom-call | bytes 1024 | tf_op jit(solution)/shard_map/project/pallas_call | solution.py:138
  114.2 5.4 %collective-permute-done.11 = f32[1,128]{1,0:T(1,128)S(1)} collective-permute-done((f32[1,128]{1,0:T(1,128)S(1)}, f32[1,128]{1,0:T(1,128)S(1)}, u32[]{:S(2)}, u32[]{:S(2)}) %collective-permute-start.11) | collective-permute-done | bytes 544 | tf_op jit(solution)/shard_map/ppermute | solution.py:20
  120.2 11.2 %collective-permute-done.7 = bf16[256,1024]{1,0:T(8,128)(2,1)} collective-permute-done((bf16[256,1024]{1,0:T(8,128)(2,1)S(1)}, bf16[256,1024]{1,0:T(8,128)(2,1)}, u32[]{:S(2)}, u32[]{:S(2)}) %collective-permute-start.7) | collective-permute-done | bytes 524320 | tf_op jit(solution)/shard_map/ppermute | solution.py:20
  144.6 12.1 %collective-permute-done.16 = bf16[256,1024]{1,0:T(8,128)(2,1)S(1)} collective-permute-done((bf16[256,1024]{1,0:T(8,128)(2,1)S(1)}, bf16[256,1024]{1,0:T(8,128)(2,1)S(1)}, u32[]{:S(2)}, u32[]{:S(2)}) %collective-permute-start.16) | collective-permute-done | bytes 524320 | tf_op jit(solution)/shard_map/ppermute | solution.py:20
  156.6 10.2 %collective-permute-done.15 = bf16[256,1024]{1,0:T(8,128)(2,1)S(1)} collective-permute-done((bf16[256,1024]{1,0:T(8,128)(2,1)S(1)}, bf16[256,1024]{1,0:T(8,128)(2,1)S(1)}, u32[]{:S(2)}, u32[]{:S(2)}) %collective-permute-start.15) | collective-permute-done | bytes 524320 | tf_op jit(solution)/shard_map/ppermute | solution.py:20
  171.3 4.9 %combine.3 = (bf16[256,1024]{1,0:T(8,128)(2,1)S(1)}, bf16[256,1024]{1,0:T(8,128)(2,1)S(1)}, f32[1,256]{1,0:T(1,128)S(1)}) custom-call(s32[6]{0:T(128)S(1)} %get-tuple-element.143.flags_ref, bf16[4,128,1024]{2,1,0:T(8,128)(2,1)S(1)} %bitcast.149, bf16[4,128,1024]{2,1,0:T(8,128)(2,1)S(1)} %collective-permute-done.18.other_ref, ...), custom_call_target="tpu_custom_call" | custom-call | bytes 1024 | tf_op jit(solution)/shard_map/combine/pallas_call | solution.py:189
  177.1 6.4 %project.6 = (bf16[4,128,1280]{2,1,0:T(8,128)(2,1)S(1)}, bf16[4,128,1280]{2,1,0:T(8,128)(2,1)S(1)}) custom-call(s32[6]{0:T(128)S(1)} %get-tuple-element.142.flags_ref, bf16[256,1024]{1,0:T(8,128)(2,1)S(1)} %get-tuple-element.59.value_ref, bf16[2,5120,1024]{2,1,0:T(8,128)(2,1)} %bitcast.163, bf16[5120,1024]{1,0:T(8,128)(2,1)} %collective-permute-done.5.got_ref), custom_call_target="tpu_custom_call" | custom-call | bytes 1024 | tf_op jit(solution)/shard_map/project/pallas_call | solution.py:138
  188.0 5.1 %project.4 = (bf16[4,128,1024]{2,1,0:T(8,128)(2,1)S(1)}, bf16[4,128,1024]{2,1,0:T(8,128)(2,1)S(1)}) custom-call(s32[6]{0:T(128)S(1)} %get-tuple-element.142.flags_ref, bf16[256,1024]{1,0:T(8,128)(2,1)S(1)} %fusion.2.value_ref.refs_0_, bf16[2,4096,1024]{2,1,0:T(8,128)(2,1)} %bitcast.168, bf16[4096,1024]{1,0:T(8,128)(2,1)} %collective-permute-done.got_ref), custom_call_target="tpu_custom_call" | custom-call | bytes 1024 | tf_op jit(solution)/shard_map/project/pallas_call | solution.py:138
  203.9 5.6 %collective-permute-done.22 = bf16[128,1024]{1,0:T(8,128)(2,1)S(1)} collective-permute-done((bf16[128,1024]{1,0:T(8,128)(2,1)S(1)}, bf16[128,1024]{1,0:T(8,128)(2,1)S(1)}, u32[]{:S(2)}, u32[]{:S(2)}) %collective-permute-start.22) | collective-permute-done | bytes 262176 | tf_op jit(solution)/shard_map/ppermute | solution.py:20
  233.5 12.0 %reduce-scatter.7.cloned.1.call-done = bf16[1,128,1024]{2,1,0:T(8,128)(2,1)} async-done(((bf16[4,128,1024]{2,1,0:T(8,128)(2,1)}), bf16[1,128,1024]{2,1,0:T(8,128)(2,1)}) %reduce-scatter.7.cloned.1.call-update) | async-done | bytes 262160 | tf_op jit(solution)/shard_map/reduce_scatter | solution.py:529
  255.4 11.5 %collective-permute-done.30 = bf16[256,1024]{1,0:T(8,128)(2,1)S(1)} collective-permute-done((bf16[256,1024]{1,0:T(8,128)(2,1)}, bf16[256,1024]{1,0:T(8,128)(2,1)S(1)}, u32[]{:S(2)}, u32[]{:S(2)}) %collective-permute-start.30) | collective-permute-done | bytes 524320 | tf_op jit(solution)/shard_map/ppermute | solution.py:20
  266.9 12.1 %collective-permute-done.29 = bf16[256,1024]{1,0:T(8,128)(2,1)S(1)} collective-permute-done((bf16[256,1024]{1,0:T(8,128)(2,1)}, bf16[256,1024]{1,0:T(8,128)(2,1)S(1)}, u32[]{:S(2)}, u32[]{:S(2)}) %collective-permute-start.29) | collective-permute-done | bytes 524320 | tf_op jit(solution)/shard_map/ppermute | solution.py:20
  294.4 6.9 %combine.4 = (bf16[256,1024]{1,0:T(8,128)(2,1)S(1)}, f32[1,1024]{1,0:T(1,128)S(1)}) custom-call(s32[6]{0:T(128)S(1)} %get-tuple-element.142.flags_ref, bf16[4,128,1280]{2,1,0:T(8,128)(2,1)S(1)} %bitcast.142, bf16[4,128,1280]{2,1,0:T(8,128)(2,1)} %collective-permute-done.31.other_ref, bf16[2,5120,1024]{2,1,0:T(8,128)(2,1)} %bitcast.164, ...), custom_call_target="tpu_custom_call" | custom-call | bytes 1024 | tf_op jit(solution)/shard_map/combine/pallas_call | solution.py:189
  301.3 5.2 %project.7 = (bf16[4,128,1024]{2,1,0:T(8,128)(2,1)S(1)}, bf16[4,128,1024]{2,1,0:T(8,128)(2,1)S(1)}) custom-call(s32[6]{0:T(128)S(1)} %get-tuple-element.143.flags_ref, bf16[256,1024]{1,0:T(8,128)(2,1)S(1)} %get-tuple-element.72.value_ref.refs_0_, bf16[2,4096,1024]{2,1,0:T(8,128)(2,1)} %bitcast.169, bf16[4096,1024]{1,0:T(8,128)(2,1)} %collective-permute-done.got_ref), custom_call_target="tpu_custom_call" | custom-call | bytes 1024 | tf_op jit(solution)/shard_map/project/pallas_call | solution.py:138
  329.9 16.5 %collective-permute-done.41 = bf16[128,1024]{1,0:T(8,128)(2,1)S(1)} collective-permute-done((bf16[128,1024]{1,0:T(8,128)(2,1)S(1)}, bf16[128,1024]{1,0:T(8,128)(2,1)S(1)}, u32[]{:S(2)}, u32[]{:S(2)}) %collective-permute-start.41) | collective-permute-done | bytes 262176 | tf_op jit(solution)/shard_map/ppermute | solution.py:20
  374.2 12.1 %collective-permute-done.46 = bf16[256,1024]{1,0:T(8,128)(2,1)S(1)} collective-permute-done((bf16[256,1024]{1,0:T(8,128)(2,1)S(1)}, bf16[256,1024]{1,0:T(8,128)(2,1)S(1)}, u32[]{:S(2)}, u32[]{:S(2)}) %collective-permute-start.46) | collective-permute-done | bytes 524320 | tf_op jit(solution)/shard_map/ppermute | solution.py:20
  404.4 6.4 %combine.5 = (bf16[256,1024]{1,0:T(8,128)(2,1)}, f32[1,1024]{1,0:T(1,128)S(1)}) custom-call(s32[6]{0:T(128)S(1)} %get-tuple-element.143.flags_ref, bf16[4,128,1280]{2,1,0:T(8,128)(2,1)S(1)} %bitcast.146, bf16[4,128,1280]{2,1,0:T(8,128)(2,1)S(1)} %collective-permute-done.51.other_ref, bf16[2,5120,1024]{2,1,0:T(8,128)(2,1)} %bitcast.165, ...), custom_call_target="tpu_custom_call" | custom-call | bytes 1024 | tf_op jit(solution)/shard_map/combine/pallas_call | solution.py:189
  443.8 7.5 %interleave.2 = bf16[1024,2,1024]{2,1,0:T(2,128)(2,1)} custom-call(s32[6]{0:T(128)S(1)} %get-tuple-element.143.flags_ref, bf16[1024,1024]{1,0:T(8,128)(2,1)S(1)} %copy-done.3, bf16[1024,1024]{1,0:T(8,128)(2,1)S(1)} %copy-done.1, bf16[1024,1024]{1,0:T(8,128)(2,1)S(1)} %collective-permute-done.56.first_ref, ...), custom_call_target="tpu_custom_call" | custom-call | bytes 1024 | tf_op jit(solution)/shard_map/interleave/pallas_call | solution.py:293
  451.3 10.0 %interleave.3 = bf16[1280,2,1024]{2,1,0:T(2,128)(2,1)} custom-call(s32[6]{0:T(128)S(1)} %get-tuple-element.143.flags_ref, bf16[1280,1024]{1,0:T(8,128)(2,1)S(1)} %outer.7.layer_0_ref, bf16[1280,1024]{1,0:T(8,128)(2,1)S(1)} %outer.4.layer_1_ref, bf16[1280,1024]{1,0:T(8,128)(2,1)S(1)} %collective-permute-done.59.first_ref, ...), custom_call_target="tpu_custom_call" | custom-call | bytes 1024 | tf_op jit(solution)/shard_map/interleave/pallas_call | solution.py:293
  (342 shorter events, 217.6 us)
Async XLA Ops:
  7.2 127.1 %reduce-scatter.5.cloned.1.call-start = ((), (), s32[]{:S(2)}) async-start(), calls=%async_computation.4 | async-start | bytes 1638400 | tf_op jit(solution)/shard_map/reduce_scatter | solution.py:529
  38.0 50.2 %collective-permute-start.5 = (bf16[5120,1024]{1,0:T(8,128)(2,1)}, bf16[5120,1024]{1,0:T(8,128)(2,1)}, u32[]{:S(2)}, u32[]{:S(2)}) collective-permute-start(bf16[5120,1024]{1,0:T(8,128)(2,1)} %dynamic-slice_bitcast_fusion), channel_id=1, source_target_pairs={{0,16},{16,0},{1,17},{17,1},{2,18},{18,2},{3,19},{19,3},{4,20},{20... | collective-permute-start | bytes 31457288 | tf_op jit(solution)/shard_map/ppermute | solution.py:20
  38.5 34.7 %collective-permute-start.1 = (bf16[2,128,1024]{2,1,0:T(8,128)(2,1)S(1)}, bf16[2,128,1024]{2,1,0:T(8,128)(2,1)S(1)}, u32[]{:S(2)}, u32[]{:S(2)}) collective-permute-start(bf16[2,128,1024]{2,1,0:T(8,128)(2,1)S(1)} %pad_maximum_fusion.8), channel_id=1, source_target_pairs={{0,12},{4,0},{8,4},{12,8},{1,13},{5,1},{9,5},{13,9},{2,14},{6,2},{... | collective-permute-start | bytes 1572872 | tf_op jit(solution)/shard_map/ppermute | solution.py:20
  41.9 31.3 %collective-permute-start.2 = (bf16[2,128,1024]{2,1,0:T(8,128)(2,1)S(1)}, bf16[2,128,1024]{2,1,0:T(8,128)(2,1)S(1)}, u32[]{:S(2)}, u32[]{:S(2)}) collective-permute-start(bf16[2,128,1024]{2,1,0:T(8,128)(2,1)S(1)} %pad_maximum_fusion.8), channel_id=1, source_target_pairs={{0,8},{4,12},{8,0},{12,4},{1,9},{5,13},{9,1},{13,5},{2,10},{6,14},... | collective-permute-start | bytes 1572872 | tf_op jit(solution)/shard_map/ppermute | solution.py:20
  66.5 100.7 %collective-permute-start = (bf16[4096,1024]{1,0:T(8,128)(2,1)}, bf16[4096,1024]{1,0:T(8,128)(2,1)}, u32[]{:S(2)}, u32[]{:S(2)}) collective-permute-start(bf16[4096,1024]{1,0:T(8,128)(2,1)} %dynamic-slice_bitcast_fusion.1), channel_id=1, source_target_pairs={{0,16},{16,0},{1,17},{17,1},{2,18},{18,2},{3,19},{19,3},{4,20},{20... | collective-permute-start | bytes 25165832 | tf_op jit(solution)/shard_map/ppermute | solution.py:20
  99.1 68.1 %all-gather.9.cloned.1.call-start = ((), (), s32[]{:S(2)}) async-start(), calls=%async_computation.8 | async-start | bytes 1310720 | tf_op jit(solution)/shard_map/all_gather | solution.py:539
  106.9 24.5 %collective-permute-start.7 = (bf16[256,1024]{1,0:T(8,128)(2,1)S(1)}, bf16[256,1024]{1,0:T(8,128)(2,1)}, u32[]{:S(2)}, u32[]{:S(2)}) collective-permute-start(bf16[256,1024]{1,0:T(8,128)(2,1)S(1)} %multiply_convert_fusion.value_ref), channel_id=1, source_target_pairs={{0,4},{4,8},{8,12},{12,0},{1,5},{5,9},{9,13},{13,1},{2,6},{6,10},{... | collective-permute-start | bytes 1572872 | tf_op jit(solution)/shard_map/ppermute | solution.py:20
  141.2 86.1 %reduce-scatter.9.cloned.1.call-start = ((), (), s32[]{:S(2)}) async-start(), calls=%async_computation.6 | async-start | bytes 1638400 | tf_op jit(solution)/shard_map/reduce_scatter | solution.py:529
  142.1 24.8 %collective-permute-start.15 = (bf16[256,1024]{1,0:T(8,128)(2,1)S(1)}, bf16[256,1024]{1,0:T(8,128)(2,1)S(1)}, u32[]{:S(2)}, u32[]{:S(2)}) collective-permute-start(bf16[256,1024]{1,0:T(8,128)(2,1)S(1)} %fusion.2.value_ref.refs_0_), channel_id=1, source_target_pairs={{0,8},{4,12},{8,0},{12,4},{1,9},{5,13},{9,1},{13,5},{2,10},{6,14},... | collective-permute-start | bytes 1572872 | tf_op jit(solution)/shard_map/ppermute | solution.py:20
  143.6 23.3 %collective-permute-start.14 = (bf16[256,1024]{1,0:T(8,128)(2,1)S(1)}, bf16[256,1024]{1,0:T(8,128)(2,1)S(1)}, u32[]{:S(2)}, u32[]{:S(2)}) collective-permute-start(bf16[256,1024]{1,0:T(8,128)(2,1)S(1)} %fusion.2.value_ref.refs_0_), channel_id=1, source_target_pairs={{0,4},{4,8},{8,12},{12,0},{1,5},{5,9},{9,13},{13,1},{2,6},{6,10},{... | collective-permute-start | bytes 1572872 | tf_op jit(solution)/shard_map/ppermute | solution.py:20
  188.0 57.5 %reduce-scatter.7.cloned.1.call-start = ((), (), s32[]{:S(2)}) async-start(), calls=%async_computation.5 | async-start | bytes 1310720 | tf_op jit(solution)/shard_map/reduce_scatter | solution.py:529
  197.3 86.0 %all-gather.11.cloned.1.call-start = ((), (), s32[]{:S(2)}) async-start(), calls=%async_computation.9 | async-start | bytes 1638400 | tf_op jit(solution)/shard_map/all_gather | solution.py:539
  251.8 63.3 %all-gather.13.cloned.1.call-start = ((), (), s32[]{:S(2)}) async-start(), calls=%async_computation.10 | async-start | bytes 1310720 | tf_op jit(solution)/shard_map/all_gather | solution.py:539
  254.3 24.7 %collective-permute-start.29 = (bf16[256,1024]{1,0:T(8,128)(2,1)}, bf16[256,1024]{1,0:T(8,128)(2,1)S(1)}, u32[]{:S(2)}, u32[]{:S(2)}) collective-permute-start(bf16[256,1024]{1,0:T(8,128)(2,1)} %copy-done.16), channel_id=1, source_target_pairs={{0,8},{4,12},{8,0},{12,4},{1,9},{5,13},{9,1},{13,5},{2,10},{6,14},... | collective-permute-start | bytes 1572872 | tf_op jit(solution)/shard_map/ppermute | solution.py:20
  254.8 24.2 %collective-permute-start.28 = (bf16[256,1024]{1,0:T(8,128)(2,1)}, bf16[256,1024]{1,0:T(8,128)(2,1)S(1)}, u32[]{:S(2)}, u32[]{:S(2)}) collective-permute-start(bf16[256,1024]{1,0:T(8,128)(2,1)} %copy-done.16), channel_id=1, source_target_pairs={{0,4},{4,8},{8,12},{12,0},{1,5},{5,9},{9,13},{13,1},{2,6},{6,10},{... | collective-permute-start | bytes 1572872 | tf_op jit(solution)/shard_map/ppermute | solution.py:20
  286.8 60.4 %reduce-scatter.11.cloned.1.call-start = ((), (), s32[]{:S(2)}) async-start(), calls=%async_computation.7 | async-start | bytes 1310720 | tf_op jit(solution)/shard_map/reduce_scatter | solution.py:529
  310.7 81.4 %all-gather.15.cloned.1.call-start = ((), (), s32[]{:S(2)}) async-start(), calls=%async_computation.11 | async-start | bytes 1638400 | tf_op jit(solution)/shard_map/all_gather | solution.py:539
  321.0 25.4 %collective-permute-start.37 = (bf16[128,1280]{1,0:T(8,128)(2,1)S(1)}, bf16[128,1280]{1,0:T(8,128)(2,1)}, u32[]{:S(2)}, u32[]{:S(2)}) collective-permute-start(bf16[128,1280]{1,0:T(8,128)(2,1)S(1)} %get-tuple-element.117), channel_id=1, source_target_pairs={{0,4},{4,8},{8,12},{12,0},{1,5},{5,9},{9,13},{13,1},{2,6},{6,10},{... | collective-permute-start | bytes 983048 | tf_op jit(solution)/shard_map/ppermute | solution.py:20
  322.5 23.9 %collective-permute-start.38 = (bf16[128,1280]{1,0:T(8,128)(2,1)S(1)}, bf16[128,1280]{1,0:T(8,128)(2,1)}, u32[]{:S(2)}, u32[]{:S(2)}) collective-permute-start(bf16[128,1280]{1,0:T(8,128)(2,1)S(1)} %get-tuple-element.116), channel_id=1, source_target_pairs={{0,8},{4,12},{8,0},{12,4},{1,9},{5,13},{9,1},{13,5},{2,10},{6,14},... | collective-permute-start | bytes 983048 | tf_op jit(solution)/shard_map/ppermute | solution.py:20
  323.1 24.1 %collective-permute-start.39 = (bf16[128,1280]{1,0:T(8,128)(2,1)S(1)}, bf16[128,1280]{1,0:T(8,128)(2,1)}, u32[]{:S(2)}, u32[]{:S(2)}) collective-permute-start(bf16[128,1280]{1,0:T(8,128)(2,1)S(1)} %get-tuple-element.115), channel_id=1, source_target_pairs={{0,12},{4,0},{8,4},{12,8},{1,13},{5,1},{9,5},{13,9},{2,14},{6,2},{... | collective-permute-start | bytes 983048 | tf_op jit(solution)/shard_map/ppermute | solution.py:20
  361.4 24.9 %collective-permute-start.46 = (bf16[256,1024]{1,0:T(8,128)(2,1)S(1)}, bf16[256,1024]{1,0:T(8,128)(2,1)S(1)}, u32[]{:S(2)}, u32[]{:S(2)}) collective-permute-start(bf16[256,1024]{1,0:T(8,128)(2,1)S(1)} %copy-done.10), channel_id=1, source_target_pairs={{0,8},{4,12},{8,0},{12,4},{1,9},{5,13},{9,1},{13,5},{2,10},{6,14},... | collective-permute-start | bytes 1572872 | tf_op jit(solution)/shard_map/ppermute | solution.py:20
  362.9 23.4 %collective-permute-start.45 = (bf16[256,1024]{1,0:T(8,128)(2,1)S(1)}, bf16[256,1024]{1,0:T(8,128)(2,1)S(1)}, u32[]{:S(2)}, u32[]{:S(2)}) collective-permute-start(bf16[256,1024]{1,0:T(8,128)(2,1)S(1)} %copy-done.10), channel_id=1, source_target_pairs={{0,4},{4,8},{8,12},{12,0},{1,5},{5,9},{9,13},{13,1},{2,6},{6,10},{... | collective-permute-start | bytes 1572872 | tf_op jit(solution)/shard_map/ppermute | solution.py:20
  416.0 35.3 %collective-permute-start.59 = (bf16[1280,1024]{1,0:T(8,128)(2,1)S(1)}, bf16[1280,1024]{1,0:T(8,128)(2,1)S(1)}, u32[]{:S(2)}, u32[]{:S(2)}) collective-permute-start(bf16[1280,1024]{1,0:T(8,128)(2,1)S(1)} %outer.4.layer_1_ref), channel_id=1, source_target_pairs={{0,16},{1,17},{2,18},{3,19},{4,20},{5,21},{6,22},{7,23},{8,24},{9,... | collective-permute-start | bytes 7864328 | tf_op jit(solution)/shard_map/ppermute | solution.py:668
  422.5 28.8 %collective-permute-start.60 = (bf16[1280,1024]{1,0:T(8,128)(2,1)S(1)}, bf16[1280,1024]{1,0:T(8,128)(2,1)}, u32[]{:S(2)}, u32[]{:S(2)}) collective-permute-start(bf16[1280,1024]{1,0:T(8,128)(2,1)S(1)} %outer.7.layer_0_ref), channel_id=1, source_target_pairs={{16,0},{17,1},{18,2},{19,3},{20,4},{21,5},{22,6},{23,7},{24,8},{25... | collective-permute-start | bytes 7864328 | tf_op jit(solution)/shard_map/ppermute | solution.py:669
  (96 other events, 575.6 us)
Sparse Core Ops, SparseCore 0:
  99.2 31.5 reduce-scatter.4
  141.3 24.3 all-gather.8
  188.1 29.1 reduce-scatter.8
  219.5 25.9 reduce-scatter.6
  251.9 31.3 all-gather.10
  286.9 28.1 all-gather.12
  317.4 26.6 reduce-scatter.10
  353.6 34.7 all-gather.14
